TPU v7x, 32 devices: a whole 2x2x4 slice. The times are simulated.
32 devices in a mesh: slab: 32 (over z, y, x, core).
Axes of the slice: x: 2, y: 2, z: 4, core: 2. Of those that a mesh axis runs over, the one named last changes fastest.
Arguments:
- tensor: float32 [128, 1024, 512], P('slab'), may hold values from 0 to 1024
- first: float32 [128, 512], P('slab'), may hold values from 0.01 to 2.01
- second: float32 [1024, 512], replicated, may hold values from 0.01 to 2.01
- third: float32 [512, 512], replicated, may hold values from 0.01 to 2.01
Outputs:
- new_first: float32 [128, 512], P('slab')
- new_second: float32 [1024, 512], P('slab')
- new_third: float32 [512, 512], P('slab')
All inputs are finite; a program needn't handle non-finite values.
Results may differ from a plain program's by a relative error of at most 0.0002.
Values sent between devices are 32-bit elements; how exact they have to be, the bound alone decides.
No kernel may reach another device: no remote copies, remote signals or barrier semaphores. Data moves between devices by JAX's collectives and lax.ppermute only.
A program may use at most 64 MiB of HBM per device.

v0:
```python
import jax
import jax.numpy as jnp
from jax import lax
from jax.sharding import PartitionSpec as P


def update(start_rows, sums, gram):
    highest = lax.Precision.HIGHEST
    lipschitz = jnp.max(jnp.sum(gram, axis=1))
    previous = start_rows
    extrapolated = start_rows
    updated = start_rows
    for turn in range(4):
        gradient = jnp.dot(extrapolated, gram, precision=highest) - sums
        updated = jnp.maximum(extrapolated - gradient / lipschitz, 0.0)
        extrapolated = updated + turn / (turn + 3.0) * (updated - previous)
        previous = updated
    return updated


def body(tensor, first, second, third):
    highest = lax.Precision.HIGHEST
    devices_count = lax.axis_size("slab")
    device_index = lax.axis_index("slab")
    second_count = second.shape[0] // devices_count
    third_count = third.shape[0] // devices_count
    gram_second = jnp.dot(second.T, second, precision=highest)
    gram_third = jnp.dot(third.T, third, precision=highest)
    partial_value = jnp.einsum("ijk,kr->ijr", tensor, third, precision=highest)
    first_sums = jnp.einsum("ijr,jr->ir", partial_value, second, precision=highest)
    new_first = update(first, first_sums, gram_second * gram_third)
    own_gram = jnp.dot(new_first.T, new_first, precision=highest)
    gram_first = lax.psum(own_gram, "slab")
    own_term = jnp.einsum("ijr,ir->jr", partial_value, new_first, precision=highest)
    second_sums = lax.psum(own_term, "slab")
    whole_second = update(second, second_sums, gram_first * gram_third)
    weighted = whole_second[None, :, :] * new_first[:, None, :]
    third_sums = jnp.einsum("ijk,ijr->kr", tensor, weighted, precision=highest)
    gram_new_second = jnp.dot(whole_second.T, whole_second, precision=highest)
    out_second = lax.dynamic_slice_in_dim(
        whole_second, device_index * second_count, second_count, 0
    )
    third_rows = lax.psum_scatter(third_sums, "slab", scatter_dimension=0, tiled=True)
    own_third = lax.dynamic_slice_in_dim(third, device_index * third_count, third_count, 0)
    new_third = update(own_third, third_rows, gram_first * gram_new_second)
    return (new_first, out_second, new_third)


def solution(mesh):
    in_specs = (P("slab", None, None), P("slab", None), P(), P())
    out_specs = (P("slab", None), P("slab", None), P("slab", None))
    return jax.shard_map(body, mesh=mesh, in_specs=in_specs, out_specs=out_specs, check_vma=False)
```

profile of v0, /device:TPU:0, one launch (start us, length us, event | category | flops | bytes accessed | tf_op | source)
XLA Modules:
  0.0 380.0 jit_solution(14814584285607130259)
XLA Ops:
  7.2 0.0 copy-start
  7.2 0.0 all-reduce.3.cloned.1.call-start
  7.2 3.5 fusion.82
  10.8 0.0 copy-done
  10.8 0.0 copy-start.1
  10.8 3.6 fusion.80
  14.4 0.0 copy-done.1
  14.4 0.6 reduce_max.27
  15.0 0.0 copy-start.7
  15.0 16.6 %multiply_reduce_fusion.1 = (f32[512,4]{0,1:T(4,128)S(1)}, f32[4,1024,512]{2,1,0:T(8,128)S(1)}) fusion(f32[512,1024]{0,1:T(8,128)S(1)} %bitcast.64, f32[4,1024,512]{2,1,0:T(8,128)} %param.4, f32[512,512]{1,0:T(8,128)} %param.7), kind=kOutput, calls=%fused_computation.1 | convolution fusion | flops 12889094144 | bytes 19931136 | tf_op jit(solution)/shard_map/ijk,kr->ijr/dot_general | solution.py:29
  31.6 0.0 copy-done.7
  31.7 1.6 fusion.35
  33.3 1.6 fusion.31
  34.9 1.6 fusion.28
  36.5 1.6 fusion.25
  38.2 0.0 copy-start.6
  38.2 2.1 fusion.83
  40.3 2.5 multiply_reduce_fusion
  42.8 2.9 copy.28
  45.7 0.0 all-reduce.3.cloned.1.call-update
  45.7 0.0 copy-start.2
  45.7 0.0 reduce-scatter.2.cloned.1.call-start
  45.8 1.9 copy.8
  47.6 139.1 %all-reduce.3.cloned.1.call-done = (f32[1024,512]{0,1:T(8,128)}, f32[512,512]{0,1:T(8,128)}) async-done(((f32[1024,512]{0,1:T(8,128)}, f32[512,512]{0,1:T(8,128)}), (f32[1024,512]{0,1:T(8,128)}, f32[512,512]{0,1:T(8,128)})) %all-reduce.3.cloned.1.call-update) | async-done | bytes 3145744 | tf_op jit(solution)/shard_map/psum | solution.py:35
  186.7 0.0 copy-done.2
  186.7 2.4 fusion.79
  189.1 0.6 reduce_max.28
  189.7 0.0 copy-start.3
  189.7 0.0 copy-start.4
  189.7 8.0 %fusion.6 = f32[1024,512]{0,1:T(8,128)S(1)} fusion(f32[1024,512]{0,1:T(8,128)} %copy.8, f32[1024,512]{0,1:T(8,128)} %get-tuple-element.6, f32[512,512]{0,1:T(8,128)} %get-tuple-element.9, f32[1024,512]{1,0:T(8,128)S(1)} %copy-done, f32[]{:T(128)} %reduce_max.28), kind=kOutput, calls=%fused_computation.9 | convolution fusion | flops 3223322624 | bytes 9437188 | tf_op jit(solution)/shard_map/dot_general | solution.py:14
  197.7 0.0 copy-done.3
  197.7 0.0 copy-done.4
  197.7 0.0 copy-start.8
  197.7 0.0 slice-start
  197.7 3.7 fusion.40
  201.5 0.0 copy-done.8
  201.5 0.0 slice-start.1
  201.5 6.0 %multiply_add_fusion = f32[1024,512]{0,1:T(8,128)S(1)} fusion(f32[1024,512]{0,1:T(8,128)S(1)} %copy-done.8, f32[1024,512]{0,1:T(8,128)S(1)} %fusion.6, f32[512,512]{0,1:T(8,128)S(1)} %copy-done.4, f32[1024,512]{0,1:T(8,128)S(1)} %fusion.40, f32[1024,512]{0,1:T(8,128)S(1)} %copy-done.3, f32[]{:T(128)} %reduce_max.28), kind=kOutput, calls=%fused_computation.11 | convolution fusion | flops 3235381248 | bytes 11534340 | tf_op jit(solution)/shard_map/dot_general | solution.py:14
  207.5 4.6 %subtract_maximum_fusion = f32[1024,512]{0,1:T(8,128)S(1)} fusion(f32[1024,512]{0,1:T(8,128)S(1)} %multiply_add_fusion, f32[1024,512]{0,1:T(8,128)S(1)} %copy-done.8, f32[512,512]{0,1:T(8,128)S(1)} %copy-done.4, f32[]{:T(128)} %reduce_max.28), kind=kOutput, calls=%fused_computation.10 | convolution fusion | flops 3223322624 | bytes 7340036 | tf_op jit(solution)/shard_map/dot_general | solution.py:14
  212.1 0.0 copy-done.6
  212.2 0.0 slice-done
  212.2 0.0 slice-done.1
  212.2 16.2 %fusion.8 = f32[512,512]{1,0:T(8,128)} fusion(f32[4,1024,512]{2,1,0:T(8,128)S(1)} %bitcast.66, f32[4,512]{1,0:T(4,128)S(1)} %fusion.25, f32[1024,512]{0,1:T(8,128)S(1)} %subtract_maximum_fusion), kind=kOutput, calls=%fused_computation.16 | convolution fusion | flops 12886999040 | bytes 11542528 | tf_op jit(solution)/shard_map/ijk,ijr->kr/dot_general | solution.py:38
  228.3 0.0 reduce-scatter.2.cloned.1.call-update
  228.4 4.7 %fusion.81 = (f32[512]{0:T(512)S(1)}, f32[512,512]{0,1:T(8,128)S(1)}) fusion(f32[512,512]{0,1:T(8,128)} %get-tuple-element.7, f32[1024,512]{0,1:T(8,128)S(1)} %subtract_maximum_fusion), kind=kOutput, calls=%fused_computation.98 | convolution fusion | flops 3221749248 | bytes 4196352 | tf_op jit(solution)/shard_map/dot_general | solution.py:39
  233.1 0.6 reduce_max.29
  233.7 0.1 constant_dynamic-slice_fusion
  233.9 0.7 copy.14
  234.6 129.6 %reduce-scatter.2.cloned.1.call-done = f32[16,512]{1,0:T(8,128)} async-done(((f32[512,512]{1,0:T(8,128)}), f32[16,512]{1,0:T(8,128)}) %reduce-scatter.2.cloned.1.call-update) | async-done | bytes 32784 | tf_op jit(solution)/shard_map/reduce_scatter | solution.py:43
  364.2 0.0 copy-start.5
  364.2 2.5 fusion.22
  366.6 2.4 fusion.19
  369.1 0.0 copy-done.5
  369.1 1.6 fusion.16
  370.7 2.2 fusion.13
  (1 shorter events, 0.0 us)
Async XLA Ops:
  7.2 3.6 copy-start
  7.2 179.5 %all-reduce.3.cloned.1.call-start = ((), (), s32[]{:S(2)}) async-start(), calls=%async_computation.2 | async-start | bytes 6291456 | tf_op jit(solution)/shard_map/psum | solution.py:35
  10.8 3.6 copy-start.1
  15.0 16.6 %copy-start.7 = (f32[4,512]{1,0:T(4,128)S(1)}, f32[4,512]{1,0:T(4,128)}, u32[]{:S(2)}) copy-start(f32[4,512]{1,0:T(4,128)} %param.5) | copy-start | bytes 24580
  38.2 174.0 %copy-start.6 = (f32[4,512]{1,0:T(4,128)}, f32[4,512]{1,0:T(4,128)S(1)}, u32[]{:S(2)}) copy-start(f32[4,512]{1,0:T(4,128)S(1)} %fusion.25) | copy-start | bytes 24580
  45.7 141.0 %copy-start.2 = (f32[512,512]{0,1:T(8,128)S(1)}, f32[512,512]{0,1:T(8,128)}, u32[]{:S(2)}) copy-start(f32[512,512]{0,1:T(8,128)} %copy-done.1) | copy-start | bytes 3145732
  45.7 318.5 %reduce-scatter.2.cloned.1.call-start = ((), (), s32[]{:S(2)}) async-start(), calls=%async_computation.1 | async-start | bytes 1081344 | tf_op jit(solution)/shard_map/reduce_scatter | solution.py:43
  189.7 8.0 %copy-start.3 = (f32[1024,512]{0,1:T(8,128)S(1)}, f32[1024,512]{0,1:T(8,128)}, u32[]{:S(2)}) copy-start(f32[1024,512]{0,1:T(8,128)} %copy.8) | copy-start | bytes 6291460
  189.7 8.0 %copy-start.4 = (f32[512,512]{0,1:T(8,128)S(1)}, f32[512,512]{0,1:T(8,128)}, u32[]{:S(2)}) copy-start(f32[512,512]{0,1:T(8,128)} %get-tuple-element.9) | copy-start | bytes 3145732
  197.7 3.8 copy-start.8
  197.7 14.4 %slice-start = ((s8[8388608]{0:T(1024)(128)(4,1)}), s8[4194304]{0:T(1024)(128)(4,1)S(1)}, s32[]{:S(2)}) async-start(s8[8388608]{0:T(1024)(128)(4,1)} %bitcast.65), calls=%async_computation.3 | async-start | bytes 8388608
  201.5 10.7 %slice-start.1 = ((s8[8388608]{0:T(1024)(128)(4,1)}), s8[4194304]{0:T(1024)(128)(4,1)S(1)}, s32[]{:S(2)}) async-start(s8[8388608]{0:T(1024)(128)(4,1)} %bitcast.65), calls=%async_computation.4 | async-start | bytes 8388608
  364.2 4.9 %copy-start.5 = (f32[16,512]{1,0:T(8,128)S(1)}, f32[16,512]{1,0:T(8,128)}, u32[]{:S(2)}) copy-start(f32[16,512]{1,0:T(8,128)} %reduce-scatter.2.cloned.1.call-done) | copy-start | bytes 98308
Sparse Core Ops, SparseCore 0:
  45.8 140.8 all-reduce.2
  228.5 135.6 reduce-scatter.1
where the time goes:
time: 385 us; the launch traced here: 380 us
  waiting for transfers between devices  269 us (70%)
  matrix products  84.4 us (22%)
  between operations  14.5 us (4%)
  other arithmetic  6.73 us (2%)
  local copies, waits for them, and re-layouts  5.68 us (1%)
    psum x1, waiting for transfers between devices, body(): second_sums = lax.psum(own_term, 'slab')  139 us
    reduce_scatter x1, waiting for transfers between devices, body(): lax.psum_scatter(third_sums, 'slab', scatter_dimension=0, tiled=True)  130 us
    dot_general x12, matrix products, update(): gradient = jnp.dot(extrapolated, gram, precision=highest) - sums  37.6 us
    dot_general x1, matrix products, body(): partial_value = jnp.einsum('ijk,kr->ijr', tensor, third, precision=highest)  16.6 us
    dot_general x1, matrix products, body(): third_sums = jnp.einsum('ijk,ijr->kr', tensor, weighted, precision=highest)  16.2 us
  transfers between devices with their start and end apart: 2, of which 2 were waited for; matrix products, arithmetic and copies ran while one was open for 2% of the time, Pallas kernels for 0%

commit v1 on v0

--- a/solution.py
+++ b/solution.py
@@ -32,7 +32,11 @@
     own_gram = jnp.dot(new_first.T, new_first, precision=highest)
     gram_first = lax.psum(own_gram, "slab")
     own_term = jnp.einsum("ijr,ir->jr", partial_value, new_first, precision=highest)
-    second_sums = lax.psum(own_term, "slab")
+    second_sums = own_term
+    for hop in (1, 2, 4, 8, 16):
+        second_sums = second_sums + lax.ppermute(
+            second_sums, "slab", [(dev, dev ^ hop) for dev in range(32)]
+        )
     whole_second = update(second, second_sums, gram_first * gram_third)
     weighted = whole_second[None, :, :] * new_first[:, None, :]
     third_sums = jnp.einsum("ijk,ijr->kr", tensor, weighted, precision=highest)

time: 385 us -> 598 us (1.55)
  waiting for transfers between devices: 269 us -> 461 us
  starting transfers between devices: 0.08 us -> 9.27 us
  matrix products: 84.4 us -> 90.6 us
    ppermute x0 -> x5, waiting for transfers between devices: none -> 140 us  [body(): lax.ppermute(second_sums, 'slab', [(dev, dev ^ hop) for dev in range(32)])]
    psum x1, waiting for transfers between devices: 139 us -> 194 us  [body(): gram_first = lax.psum(own_gram, 'slab')]
    ppermute x0 -> x5, starting transfers between devices: none -> 9.19 us  [body(): lax.ppermute(second_sums, 'slab', [(dev, dev ^ hop) for dev in range(32)])]
  transfers between devices with their start and end apart: 2 -> 7, of which waited for: 2 -> 6; matrix products, arithmetic and copies ran while one was open for 2% -> 2% of each run, Pallas kernels for 0% -> 0%
where the time goes in v1:
time: 598 us; the launch traced here: 593 us
  waiting for transfers between devices  461 us (77%)
  matrix products  90.6 us (15%)
  between operations  14.5 us (2%)
  other arithmetic  11.1 us (2%)
  starting transfers between devices  9.27 us (2%)
  local copies, waits for them, and re-layouts  7 us (1%)
    psum x1, waiting for transfers between devices, body(): gram_first = lax.psum(own_gram, 'slab')  194 us
    ppermute x5, waiting for transfers between devices, body(): lax.ppermute(second_sums, 'slab', [(dev, dev ^ hop) for dev in range(32)])  140 us
    reduce_scatter x1, waiting for transfers between devices, body(): lax.psum_scatter(third_sums, 'slab', scatter_dimension=0, tiled=True)  127 us
    dot_general x12, matrix products, update(): gradient = jnp.dot(extrapolated, gram, precision=highest) - sums  42.8 us
    dot_general x1, matrix products, body(): partial_value = jnp.einsum('ijk,kr->ijr', tensor, third, precision=highest)  16.6 us
    dot_general x1, matrix products, body(): third_sums = jnp.einsum('ijk,ijr->kr', tensor, weighted, precision=highest)  16.2 us
  transfers between devices with their start and end apart: 7, of which 6 were waited for; matrix products, arithmetic and copies ran while one was open for 2% of the time, Pallas kernels for 0%

profile of v1, /device:TPU:0, one launch (start us, length us, event | category | flops | bytes accessed | tf_op | source)
XLA Modules:
  0.0 593.4 jit_solution(1148539454076565331)
XLA Ops:
  7.2 0.0 copy-start
  7.2 0.0 all-reduce.2.cloned.1.call-start
  7.2 3.5 fusion.83
  10.8 0.0 copy-done
  10.8 0.0 copy-start.3
  10.8 3.6 fusion.81
  14.4 0.0 copy-done.3
  14.4 0.6 reduce_max.27
  15.0 16.6 %multiply_reduce_fusion.1 = (f32[512,4]{0,1:T(4,128)S(1)}, f32[4,1024,512]{2,1,0:T(8,128)S(1)}) fusion(f32[512,1024]{0,1:T(8,128)S(1)} %bitcast.65, f32[4,1024,512]{2,1,0:T(8,128)} %param.4, f32[512,512]{1,0:T(8,128)} %param.7), kind=kOutput, calls=%fused_computation.1 | convolution fusion | flops 12889094144 | bytes 19931136 | tf_op jit(solution)/shard_map/ijk,kr->ijr/dot_general | solution.py:29
  31.6 0.0 copy-done.7
  31.7 1.6 fusion.35
  33.3 1.6 fusion.31
  34.9 1.6 fusion.28
  36.5 1.6 fusion.25
  38.2 0.0 copy-start.6
  38.2 2.5 multiply_reduce_fusion
  40.7 3.3 copy.28
  44.0 0.6 collective-permute-start
  44.6 4.0 collective-permute-done
  48.6 2.0 bitcast_add_fusion
  50.5 2.9 collective-permute-start.1
  53.5 45.9 %collective-permute-done.1 = f32[1024,512]{0,1:T(8,128)S(1)} collective-permute-done((f32[1024,512]{0,1:T(8,128)S(1)}, f32[1024,512]{0,1:T(8,128)S(1)}, u32[]{:S(2)}, u32[]{:S(2)}) %collective-permute-start.1) | collective-permute-done | bytes 2097184 | tf_op jit(solution)/shard_map/ppermute | solution.py:37
  99.4 0.6 add.56
  99.9 1.8 collective-permute-start.2
  101.8 45.3 %collective-permute-done.2 = f32[1024,512]{0,1:T(8,128)S(1)} collective-permute-done((f32[1024,512]{0,1:T(8,128)S(1)}, f32[1024,512]{0,1:T(8,128)S(1)}, u32[]{:S(2)}, u32[]{:S(2)}) %collective-permute-start.2) | collective-permute-done | bytes 2097184 | tf_op jit(solution)/shard_map/ppermute | solution.py:37
  147.1 0.6 add.57
  147.7 1.6 collective-permute-start.3
  149.3 44.7 %collective-permute-done.3 = f32[1024,512]{0,1:T(8,128)S(1)} collective-permute-done((f32[1024,512]{0,1:T(8,128)S(1)}, f32[1024,512]{0,1:T(8,128)S(1)}, u32[]{:S(2)}, u32[]{:S(2)}) %collective-permute-start.3) | collective-permute-done | bytes 2097184 | tf_op jit(solution)/shard_map/ppermute | solution.py:37
  194.0 1.7 add.58
  195.7 2.3 collective-permute-start.4
  198.0 2.1 fusion.84
  200.1 0.0 all-reduce.2.cloned.1.call-update
  200.1 0.0 reduce-scatter.2.cloned.1.call-start
  200.2 1.9 copy.8
  202.0 193.6 %all-reduce.2.cloned.1.call-done = f32[512,512]{0,1:T(8,128)} async-done(((f32[512,512]{0,1:T(8,128)}), f32[512,512]{0,1:T(8,128)}) %all-reduce.2.cloned.1.call-update) | async-done | bytes 1048592 | tf_op jit(solution)/shard_map/psum | solution.py:33
  395.6 1.8 fusion.80
  397.4 0.6 reduce_max.28
  398.0 0.0 collective-permute-done.4
  398.0 7.2 %fusion.6 = f32[1024,512]{0,1:T(8,128)S(1)} fusion(f32[1024,512]{0,1:T(8,128)} %copy.8, f32[512,512]{0,1:T(8,128)S(1)} %get-tuple-element.7, f32[1024,512]{1,0:T(8,128)S(1)} %copy-done, f32[]{:T(128)} %reduce_max.28, f32[1024,512]{0,1:T(8,128)} %add.58, f32[1024,512]{0,1:T(8,128)} %collective-permute-done.4), kind=kOutput, calls=%fused_computation.9 | convolution fusion | flops 3223846912 | bytes 11534340 | tf_op jit(solution)/shard_map/dot_general | solution.py:14
  405.2 0.0 copy-done.1
  405.2 0.0 slice-start
  405.3 3.7 fusion.40
  408.9 0.0 slice-start.1
  408.9 9.8 %multiply_add_fusion = f32[1024,512]{0,1:T(8,128)S(1)} fusion(f32[1024,512]{0,1:T(8,128)S(1)} %fusion.6, f32[512,512]{0,1:T(8,128)S(1)} %get-tuple-element.7, f32[1024,512]{0,1:T(8,128)S(1)} %fusion.40, f32[1024,512]{0,1:T(8,128)S(1)} %copy-done.1, f32[]{:T(128)} %reduce_max.28, f32[1024,512]{0,1:T(8,128)} %add.58, f32[1024,512]{0,1:T(8,128)} %collective-permute-done.4), kind=kOutput, calls=%fused_computation.11 | convolution fusion | flops 3236429824 | bytes 13631492 | tf_op jit(solution)/shard_map/dot_general | solution.py:14
  418.7 6.7 %subtract_maximum_fusion = f32[1024,512]{0,1:T(8,128)S(1)} fusion(f32[1024,512]{0,1:T(8,128)S(1)} %multiply_add_fusion, f32[512,512]{0,1:T(8,128)S(1)} %get-tuple-element.7, f32[]{:T(128)} %reduce_max.28, f32[1024,512]{0,1:T(8,128)} %add.58, f32[1024,512]{0,1:T(8,128)} %collective-permute-done.4), kind=kOutput, calls=%fused_computation.10 | convolution fusion | flops 3223846912 | bytes 9437188 | tf_op jit(solution)/shard_map/dot_general | solution.py:14
  425.5 0.0 copy-done.6
  425.5 0.0 slice-done
  425.5 0.0 slice-done.1
  425.5 0.0 copy-start.2
  425.5 0.0 copy-start.4
  425.5 16.2 %fusion.8 = f32[512,512]{1,0:T(8,128)} fusion(f32[4,1024,512]{2,1,0:T(8,128)S(1)} %bitcast.67, f32[4,512]{1,0:T(4,128)S(1)} %fusion.25, f32[1024,512]{0,1:T(8,128)S(1)} %subtract_maximum_fusion), kind=kOutput, calls=%fused_computation.16 | convolution fusion | flops 12886999040 | bytes 11542528 | tf_op jit(solution)/shard_map/ijk,ijr->kr/dot_general | solution.py:42
  441.7 0.0 copy-done.2
  441.7 0.0 reduce-scatter.2.cloned.1.call-update
  441.7 0.0 copy-done.4
  441.7 5.7 fusion.82
  447.4 0.7 reduce_max.29
  448.1 1.1 constant_dynamic-slice_fusion
  449.2 0.7 copy.14
  450.0 127.4 %reduce-scatter.2.cloned.1.call-done = f32[16,512]{1,0:T(8,128)} async-done(((f32[512,512]{1,0:T(8,128)}), f32[16,512]{1,0:T(8,128)}) %reduce-scatter.2.cloned.1.call-update) | async-done | bytes 32784 | tf_op jit(solution)/shard_map/reduce_scatter | solution.py:47
  577.3 2.5 fusion.22
  579.8 2.5 fusion.19
  582.3 0.0 copy-done.5
  582.3 1.7 fusion.16
  584.0 2.3 fusion.13
  (4 shorter events, 0.0 us)
Async XLA Ops:
  7.2 3.6 copy-start
  7.2 388.4 %all-reduce.2.cloned.1.call-start = ((), (), s32[]{:S(2)}) async-start(), calls=%async_computation.1 | async-start | bytes 2097152 | tf_op jit(solution)/shard_map/psum | solution.py:33
  10.8 3.6 copy-start.3
  15.0 16.6 %copy-start.7 = (f32[4,512]{1,0:T(4,128)S(1)}, f32[4,512]{1,0:T(4,128)}, u32[]{:S(2)}) copy-start(f32[4,512]{1,0:T(4,128)} %param.5) | copy-start | bytes 24580
  38.2 387.3 %copy-start.6 = (f32[4,512]{1,0:T(4,128)}, f32[4,512]{1,0:T(4,128)S(1)}, u32[]{:S(2)}) copy-start(f32[4,512]{1,0:T(4,128)S(1)} %fusion.25) | copy-start | bytes 24580
  44.0 4.6 collective-permute-start
  50.5 48.8 %collective-permute-start.1 = (f32[1024,512]{0,1:T(8,128)S(1)}, f32[1024,512]{0,1:T(8,128)S(1)}, u32[]{:S(2)}, u32[]{:S(2)}) collective-permute-start(f32[1024,512]{0,1:T(8,128)S(1)} %bitcast_add_fusion), channel_id=1, source_target_pairs={{0,2},{1,3},{2,0},{3,1},{4,6},{5,7},{6,4},{7,5},{8,10},{9,11},{10,... | collective-permute-start | bytes 6291464 | tf_op jit(solution)/shard_map/ppermute | solution.py:37
  99.9 47.2 %collective-permute-start.2 = (f32[1024,512]{0,1:T(8,128)S(1)}, f32[1024,512]{0,1:T(8,128)S(1)}, u32[]{:S(2)}, u32[]{:S(2)}) collective-permute-start(f32[1024,512]{0,1:T(8,128)S(1)} %add.56), channel_id=1, source_target_pairs={{0,4},{1,5},{2,6},{3,7},{4,0},{5,1},{6,2},{7,3},{8,12},{9,13},{10,... | collective-permute-start | bytes 6291464 | tf_op jit(solution)/shard_map/ppermute | solution.py:37
  147.7 46.3 %collective-permute-start.3 = (f32[1024,512]{0,1:T(8,128)S(1)}, f32[1024,512]{0,1:T(8,128)S(1)}, u32[]{:S(2)}, u32[]{:S(2)}) collective-permute-start(f32[1024,512]{0,1:T(8,128)S(1)} %add.57), channel_id=1, source_target_pairs={{0,8},{1,9},{2,10},{3,11},{4,12},{5,13},{6,14},{7,15},{8,0},{9,1},... | collective-permute-start | bytes 6291464 | tf_op jit(solution)/shard_map/ppermute | solution.py:37
  195.7 202.3 %collective-permute-start.4 = (f32[1024,512]{0,1:T(8,128)}, f32[1024,512]{0,1:T(8,128)}, u32[]{:S(2)}, u32[]{:S(2)}) collective-permute-start(f32[1024,512]{0,1:T(8,128)} %add.58), channel_id=1, source_target_pairs={{0,16},{1,17},{2,18},{3,19},{4,20},{5,21},{6,22},{7,23},{8,24},{9,... | collective-permute-start | bytes 6291464 | tf_op jit(solution)/shard_map/ppermute | solution.py:37
  200.1 377.2 %reduce-scatter.2.cloned.1.call-start = ((), (), s32[]{:S(2)}) async-start(), calls=%async_computation.2 | async-start | bytes 1081344 | tf_op jit(solution)/shard_map/reduce_scatter | solution.py:47
  398.0 7.2 %copy-start.1 = (f32[1024,512]{0,1:T(8,128)S(1)}, f32[1024,512]{0,1:T(8,128)}, u32[]{:S(2)}) copy-start(f32[1024,512]{0,1:T(8,128)} %copy.8) | copy-start | bytes 6291460
  405.2 20.2 %slice-start = ((s8[8388608]{0:T(1024)(128)(4,1)}), s8[4194304]{0:T(1024)(128)(4,1)S(1)}, s32[]{:S(2)}) async-start(s8[8388608]{0:T(1024)(128)(4,1)} %bitcast.66), calls=%async_computation.3 | async-start | bytes 8388608
  408.9 16.6 %slice-start.1 = ((s8[8388608]{0:T(1024)(128)(4,1)}), s8[4194304]{0:T(1024)(128)(4,1)S(1)}, s32[]{:S(2)}) async-start(s8[8388608]{0:T(1024)(128)(4,1)} %bitcast.66), calls=%async_computation.4 | async-start | bytes 8388608
  425.5 16.2 %copy-start.2 = (f32[1024,512]{0,1:T(8,128)}, f32[1024,512]{0,1:T(8,128)S(1)}, u32[]{:S(2)}) copy-start(f32[1024,512]{0,1:T(8,128)S(1)} %subtract_maximum_fusion) | copy-start | bytes 6291460
  425.5 16.2 %copy-start.4 = (f32[512,512]{0,1:T(8,128)S(1)}, f32[512,512]{0,1:T(8,128)}, u32[]{:S(2)}) copy-start(f32[512,512]{0,1:T(8,128)} %all-reduce.2.cloned.1.call-done) | copy-start | bytes 3145732
  577.3 5.0 copy-start.5
Sparse Core Ops, SparseCore 0:
  200.2 195.3 all-reduce.1
  441.8 135.4 reduce-scatter.1
